TPU v7x, 32 devices: a whole 2x2x4 slice. The times are simulated.
32 devices in a mesh: grp: 2 (over y), ctx: 16 (over z, x, core).
Axes of the slice: x: 2, y: 2, z: 4, core: 2. Of those that a mesh axis runs over, the one named last changes fastest.
Arguments:
- query_rows: bfloat16 [4096, 4096], P(('grp', 'ctx')), parts along dimension 0, may hold values from -6 to 6
- key_rows: bfloat16 [4096, 4096], P(('grp', 'ctx')), parts along dimension 0, may hold values from -6 to 6
- value_rows: bfloat16 [4096, 4096], P(('grp', 'ctx')), parts along dimension 0, may hold values from -6 to 6
- grad_out: bfloat16 [4096, 4096], P(('grp', 'ctx')), parts along dimension 0, may hold values from -6 to 6
- conv_filter: bfloat16 [256, 128], replicated, may hold values from -0.44194174 to 0.44194174
Outputs:
- grad_query: bfloat16 [4096, 4096], P(('grp', 'ctx')), parts along dimension 0
- grad_key: bfloat16 [4096, 4096], P(('grp', 'ctx')), parts along dimension 0
- grad_value: bfloat16 [4096, 4096], P(('grp', 'ctx')), parts along dimension 0
- grad_filter: float32 [512, 128], P(('grp', 'ctx')), parts along dimension 0
There are 2 independent parts, one for each index of `grp`. A program takes and returns all parts, laid end to end along the dimension named above; an argument that names none is the same for every part. Nothing has to cross between parts.
All inputs are finite; a program needn't handle non-finite values.
Results may differ from a plain program's by a relative error of at most 0.005.
Values may be sent and summed in bfloat16 or wider, within the bound.
No kernel may reach another device: no remote copies, remote signals or barrier semaphores. Data moves between devices by JAX's collectives and lax.ppermute only.
A program may use at most 64 MiB of HBM per device.

v0:
```python
import math
import jax
import jax.numpy as jnp
from jax import lax
from jax.sharding import PartitionSpec as P

GSIZE = 16
TAPS = 128


def toeplitz(filter_rows, offsets):
    taps_index = lax.broadcasted_iota(jnp.int32, offsets.shape + (TAPS,), 2)
    selector = (offsets[:, :, None] == taps_index).astype(filter_rows.dtype)
    picked = jnp.einsum("gj,tsj->gts", filter_rows, selector, preferred_element_type=jnp.float32)
    return picked.astype(filter_rows.dtype)


def block_terms(prod_now, prod_before, grad_now, grad_after, filter_rows):
    block_total, block_rows, channels = prod_now.shape
    rim_rows = prod_before.shape[1]
    groups_here = channels // GSIZE
    row_index = lax.broadcasted_iota(jnp.int32, (block_rows, block_rows + rim_rows), 0)
    col_index = lax.broadcasted_iota(jnp.int32, (block_rows, block_rows + rim_rows), 1)
    causal = toeplitz(filter_rows, rim_rows + row_index - col_index)
    future = toeplitz(filter_rows, col_index - row_index)
    extended = jnp.concatenate([prod_before, prod_now], axis=1).reshape(
        block_total, block_rows + rim_rows, groups_here, GSIZE
    )
    grads_ahead = jnp.concatenate([grad_now, grad_after], axis=1).reshape(
        block_total, block_rows + rim_rows, groups_here, GSIZE
    )
    mixed_sum = jnp.einsum("gts,bsgc->btgc", causal, extended, preferred_element_type=jnp.float32)
    back_sum = jnp.einsum("gts,bsgc->btgc", future, grads_ahead, preferred_element_type=jnp.float32)
    grads_here = grad_now.reshape(block_total, block_rows, groups_here, GSIZE)
    pair_sums = jnp.einsum(
        "btgc,bsgc->gts", grads_here, extended, preferred_element_type=jnp.float32
    )
    flattened = pair_sums.reshape(groups_here, block_rows * (block_rows + rim_rows))
    flattened = jnp.pad(flattened, ((0, 0), (0, block_rows)))
    skewed = flattened.reshape(groups_here, block_rows, block_rows + rim_rows + 1)
    picked = skewed[:, :, rim_rows - TAPS + 1 : rim_rows + 1]
    filter_part = jnp.flip(jnp.sum(picked, axis=1), axis=1)
    shape_out = (block_total, block_rows, channels)
    return (mixed_sum.reshape(shape_out), back_sum.reshape(shape_out), filter_part)


def window_terms(prod_now, prod_before, grad_now, grad_after, filter_rows, sub_rows):
    block_total, block_rows, channels = prod_now.shape
    sub_count = block_rows // sub_rows
    prod_full = jnp.concatenate([prod_before, prod_now], axis=1)
    prod_full = prod_full.reshape(block_total, (block_rows + TAPS) // sub_rows, sub_rows, channels)
    grad_full = jnp.concatenate([grad_now, grad_after], axis=1)
    grad_full = grad_full.reshape(block_total, (block_rows + TAPS) // sub_rows, sub_rows, channels)
    before_win = prod_full[:, 0:sub_count]
    after_win = grad_full[:, 1 : 1 + sub_count]
    flat_count = block_total * sub_count
    mixed_sum, back_sum, filter_part = block_terms(
        prod_now,
        before_win.reshape(flat_count, TAPS, channels),
        grad_now,
        after_win.reshape(flat_count, TAPS, channels),
        filter_rows,
    )
    return (mixed_sum, back_sum, filter_part)


def run_blocks(prod_now, prod_before, grad_now, grad_after, filter_rows, sub_rows):
    block_total, block_rows, channels = prod_now.shape
    block_width = min(512, channels)
    block_count = channels // block_width

    def to_blocks(array):
        return jnp.moveaxis(
            array.reshape(array.shape[0], array.shape[1], block_count, block_width), 2, 0
        )

    def from_blocks(array):
        return jnp.moveaxis(array, 0, 2).reshape(block_total, block_rows, channels)

    def one_block(block_items):
        return window_terms(
            block_items[0], block_items[1], block_items[2], block_items[3], block_items[4], sub_rows
        )

    block_items = (
        to_blocks(prod_now),
        to_blocks(prod_before),
        to_blocks(grad_now),
        to_blocks(grad_after),
        filter_rows.reshape(block_count, block_width // GSIZE, TAPS),
    )
    mixed_sum, back_sum, filter_part = lax.map(one_block, block_items)
    return (
        from_blocks(mixed_sum),
        from_blocks(back_sum),
        filter_part.reshape(channels // GSIZE, TAPS),
    )


def shards(query_rows, key_rows, value_rows, grad_out, conv_filter):
    product = (key_rows.astype(jnp.float32) * value_rows.astype(jnp.float32)).astype(jnp.bfloat16)
    gated_grad = (grad_out.astype(jnp.float32) * query_rows.astype(jnp.float32)).astype(
        jnp.bfloat16
    )
    local_rows = product.shape[0]
    moved_prod, moved_grad = (
        lax.all_to_all(product, "ctx", split_axis=1, concat_axis=0, tiled=True),
        lax.all_to_all(gated_grad, "ctx", split_axis=1, concat_axis=0, tiled=True),
    )
    total_rows, channels = moved_prod.shape
    block_total = total_rows // TAPS
    blocks_prod = moved_prod.reshape(block_total, TAPS, channels)
    blocks_grad = moved_grad.reshape(block_total, TAPS, channels)
    zero_block = jnp.zeros((1, TAPS, channels), jnp.bfloat16)
    rows_before = jnp.concatenate([zero_block, blocks_prod[:-1]], axis=0)
    rows_after = jnp.concatenate([blocks_grad[1:], zero_block], axis=0)
    groups_here = channels // GSIZE
    own_filter = lax.dynamic_slice_in_dim(
        conv_filter, lax.axis_index("ctx") * groups_here, groups_here, 0
    )
    mixed_sum, back_sum, filter_part = run_blocks(
        blocks_prod, rows_before, blocks_grad, rows_after, own_filter, TAPS
    )
    mixed_sum = mixed_sum.reshape(total_rows, channels)
    back_sum = back_sum.reshape(total_rows, channels)
    mixed_home, back_home = (
        lax.all_to_all(mixed_sum, "ctx", split_axis=0, concat_axis=1, tiled=True),
        lax.all_to_all(back_sum, "ctx", split_axis=0, concat_axis=1, tiled=True),
    )
    grad_scale = 1.0 / math.sqrt(local_rows * lax.axis_size("ctx") * GSIZE)
    grad_query = (grad_out.astype(jnp.float32) * mixed_home).astype(jnp.bfloat16)
    grad_key = (back_home * value_rows.astype(jnp.float32)).astype(jnp.bfloat16)
    grad_value = (back_home * key_rows.astype(jnp.float32)).astype(jnp.bfloat16)
    return (grad_query, grad_key, grad_value, filter_part * grad_scale)


def solution(mesh):
    return jax.shard_map(
        shards,
        mesh=mesh,
        in_specs=(
            P(("grp", "ctx"), None),
            P(("grp", "ctx"), None),
            P(("grp", "ctx"), None),
            P(("grp", "ctx"), None),
            P(),
        ),
        out_specs=(
            P(("grp", "ctx"), None),
            P(("grp", "ctx"), None),
            P(("grp", "ctx"), None),
            P(("grp", "ctx"), None),
        ),
        check_vma=False,
    )
```

profile of v0, /device:TPU:15, one launch (start us, length us, event | category | flops | bytes accessed | tf_op | source)
XLA Modules:
  0.0 199.6 jit_solution(10627907065178947283)
XLA Ops:
  0.6 0.0 copy-start
  0.6 1.8 fusion.7
  2.5 1.3 copy.47
  3.8 6.5 %all-to-all-start.2 = ((bf16[128,16,256]{0,2,1:T(8,128)(2,1)}), bf16[128,16,256]{0,2,1:T(8,128)(2,1)S(1)}, u32[]{:S(2)}, u32[]{:S(2)}) async-start(bf16[128,16,256]{0,2,1:T(8,128)(2,1)} %bitcast.11), calls=%async_computation.2 | async-start | bytes 2097152 | tf_op jit(solution)/shard_map/all_to_all | solution.py:108
  10.3 0.0 copy-done
  10.3 8.2 %fusion.26 = bf16[16,128,256,1]{2,0,1,3:T(8,128)(2,1)} fusion(s32[128,256]{1,0:T(8,128)S(1)} %iota_subtract_fusion, bf16[256,128]{1,0:T(8,128)(2,1)S(1)} %copy-done, s32[]{:T(128)S(6)} %select_n.3), kind=kOutput, calls=%fused_computation.33 | convolution fusion | flops 138936320 | bytes 1183748 | tf_op jit(solution)/shard_map/while/body/eval_jaxpr/gj,tsj->gts/dot_general | solution.py:14
  18.5 16.7 %all-to-all-done.2 = bf16[128,16,256]{0,2,1:T(8,128)(2,1)S(1)} async-done(((bf16[128,16,256]{0,2,1:T(8,128)(2,1)}), bf16[128,16,256]{0,2,1:T(8,128)(2,1)S(1)}, u32[]{:S(2)}, u32[]{:S(2)}) %all-to-all-start.2) | async-done | bytes 1048608 | tf_op jit(solution)/shard_map/all_to_all | solution.py:108
  35.2 0.1 slice.27
  35.2 0.3 fusion.11
  35.5 2.1 %reshape.111 = bf16[16,2,128,256]{2,1,3,0:T(2,128)(2,1)} reshape(bf16[16,256,256]{1,2,0:T(8,128)(2,1)S(1)} %fusion.11) | data formatting | bytes 4194304 | tf_op jit(solution)/shard_map/while/body/eval_jaxpr/reshape | solution.py:53
  37.6 4.0 %slice.28 = bf16[16,1,128,256]{2,1,3,0:T(2,128)(2,1)S(1)} slice(bf16[16,2,128,256]{2,1,3,0:T(2,128)(2,1)} %reshape.111), slice={[0:16], [1:2], [0:128], [0:256]} | slice | bytes 2097152 | tf_op jit(solution)/shard_map/while/body/eval_jaxpr/slice | solution.py:55
  41.6 0.0 copy-start.4
  41.6 0.2 copy.64
  41.8 1.0 copy-done.4
  42.8 0.7 fusion.20
  43.5 1.6 copy.52
  45.1 4.8 %all-to-all-start.3 = ((f32[16,128,256]{1,2,0:T(8,128)}), f32[16,128,256]{1,2,0:T(8,128)S(1)}, u32[]{:S(2)}, u32[]{:S(2)}) async-start(f32[16,128,256]{1,2,0:T(8,128)} %bitcast.49), calls=%async_computation.3 | async-start | bytes 4194304 | tf_op jit(solution)/shard_map/all_to_all | solution.py:128
  49.9 2.3 %copy.38 = bf16[128,4096]{0,1:T(8,128)(2,1)} copy(bf16[128,4096]{1,0:T(8,128)(2,1)} %param.6) | data formatting | bytes 2097152 | tf_op args[1]
  52.2 2.3 %copy.39 = bf16[128,4096]{0,1:T(8,128)(2,1)} copy(bf16[128,4096]{1,0:T(8,128)(2,1)} %param.7) | data formatting | bytes 2097152 | tf_op args[2]
  54.5 42.9 %all-to-all-done.3 = f32[16,128,256]{1,2,0:T(8,128)S(1)} async-done(((f32[16,128,256]{1,2,0:T(8,128)}), f32[16,128,256]{1,2,0:T(8,128)S(1)}, u32[]{:S(2)}, u32[]{:S(2)}) %all-to-all-start.3) | async-done | bytes 2097184 | tf_op jit(solution)/shard_map/all_to_all | solution.py:128
  97.4 3.6 %fusion.8 = (bf16[128,4096]{0,1:T(8,128)(2,1)}, bf16[128,4096]{0,1:T(8,128)(2,1)}, bf16[128,4096]{0,1:T(8,128)(2,1)}) fusion(bf16[128,4096]{0,1:T(8,128)(2,1)} %copy.38, f32[16,128,256]{1,2,0:T(8,128)S(1)} %all-to-all-done.3, bf16[128,4096]{0,1:T(8,128)(2,1)} %copy.39), kind=kLoop, calls=%fused_computation.17 | loop fusion | flops 4194304 | bytes 7340032 | tf_op jit(solution)/shard_map/convert_element_type | solution.py:133
  100.9 4.8 %all-to-all-start = ((bf16[128,16,256]{0,2,1:T(8,128)(2,1)}), bf16[128,16,256]{0,2,1:T(8,128)(2,1)S(1)}, u32[]{:S(2)}, u32[]{:S(2)}) async-start(bf16[128,16,256]{0,2,1:T(8,128)(2,1)} %bitcast.55), calls=%async_computation | async-start | bytes 2097152 | tf_op jit(solution)/shard_map/all_to_all | solution.py:107
  105.7 0.1 iota_subtract_fusion.1
  105.8 8.2 %fusion.25 = bf16[16,128,256,1]{2,0,1,3:T(8,128)(2,1)} fusion(s32[128,256]{1,0:T(8,128)S(1)} %iota_subtract_fusion.1, bf16[256,128]{1,0:T(8,128)(2,1)S(1)} %copy-done, s32[]{:T(128)S(6)} %select_n.3), kind=kOutput, calls=%fused_computation.32 | convolution fusion | flops 138936320 | bytes 1183748 | tf_op jit(solution)/shard_map/while/body/eval_jaxpr/gj,tsj->gts/dot_general | solution.py:14
  114.0 16.6 %all-to-all-done = bf16[128,16,256]{0,2,1:T(8,128)(2,1)S(1)} async-done(((bf16[128,16,256]{0,2,1:T(8,128)(2,1)}), bf16[128,16,256]{0,2,1:T(8,128)(2,1)S(1)}, u32[]{:S(2)}, u32[]{:S(2)}) %all-to-all-start) | async-done | bytes 1048608 | tf_op jit(solution)/shard_map/all_to_all | solution.py:107
  130.6 0.1 slice.25
  130.7 1.6 fusion.12
  132.2 3.9 %copy.40 = bf16[16,256,256]{2,1,0:T(8,128)(2,1)} copy(bf16[16,256,256]{1,2,0:T(8,128)(2,1)} %fusion.12) | data formatting | bytes 4194304 | tf_op jit(solution)/shard_map/while/body/eval_jaxpr/concatenate | solution.py:50
  136.2 2.3 %slice.26 = bf16[16,1,128,256]{3,2,1,0:T(8,128)(2,1)} slice(bf16[16,2,128,256]{3,2,1,0:T(8,128)(2,1)} %bitcast.52), slice={[0:16], [0:1], [0:128], [0:256]} | slice | bytes 2097152 | tf_op jit(solution)/shard_map/while/body/eval_jaxpr/slice | solution.py:54
  138.5 1.6 copy.41
  140.1 0.0 copy-start.2
  140.1 2.3 %fusion.17 = f32[16,128,16,16]{1,3,0,2:T(8,128)S(1)} fusion(bf16[16,128,256,1]{2,0,1,3:T(8,128)(2,1)} %fusion.25, bf16[16,128,16,16]{1,3,2,0:T(8,128)(2,1)S(1)} %bitcast.46, bf16[16,128,16,16]{1,3,2,0:T(8,128)(2,1)S(1)} %bitcast.53), kind=kOutput, calls=%fused_computation.28 | convolution fusion | flops 272629760 | bytes 5242880 | tf_op jit(solution)/shard_map/while/body/eval_jaxpr/gts,bsgc->btgc/dot_general | solution.py:32
  142.4 0.0 copy-done.2
  142.4 1.6 copy.45
  144.0 4.8 %all-to-all-start.1 = ((f32[16,128,256]{1,2,0:T(8,128)}), f32[16,128,256]{1,2,0:T(8,128)}, u32[]{:S(2)}, u32[]{:S(2)}) async-start(f32[16,128,256]{1,2,0:T(8,128)} %bitcast.48), calls=%async_computation.1 | async-start | bytes 4194304 | tf_op jit(solution)/shard_map/all_to_all | solution.py:127
  148.8 0.0 copy-start.1
  148.8 2.4 %copy.55 = bf16[128,4096]{1,0:T(8,128)(2,1)} copy(bf16[128,4096]{0,1:T(8,128)(2,1)} %get-tuple-element.26) | data formatting | bytes 2097152
  151.2 0.0 copy-done.1
  151.2 1.3 copy.54
  152.5 1.7 fusion.35
  154.2 1.2 copy.65
  155.5 0.1 pad.7
  155.6 3.6 %reshape.113 = f32[16,128,257]{2,1,0:T(8,128)} reshape(f32[16,32896]{1,0:T(8,128)S(1)} %pad.7) | data formatting | bytes 4210688 | tf_op jit(solution)/shard_map/while/body/eval_jaxpr/reshape | solution.py:40
  159.3 1.9 slice_reduce_fusion
  161.2 0.1 rev.5
  161.3 0.6 broadcast_multiply_fusion
  161.9 34.5 %all-to-all-done.1 = f32[16,128,256]{1,2,0:T(8,128)} async-done(((f32[16,128,256]{1,2,0:T(8,128)}), f32[16,128,256]{1,2,0:T(8,128)}, u32[]{:S(2)}, u32[]{:S(2)}) %all-to-all-start.1) | async-done | bytes 2097184 | tf_op jit(solution)/shard_map/all_to_all | solution.py:127
  196.4 0.0 copy-start.3
  196.4 2.0 %copy.46 = f32[128,4096]{1,0:T(8,128)S(1)} copy(f32[128,4096]{0,1:T(8,128)} %bitcast.10) | data formatting | bytes 4194304 | tf_op jit(solution)/shard_map/all_to_all | solution.py:127
  198.4 0.0 copy-done.3
  198.4 1.2 fusion.6
  (2 shorter events, 0.0 us)
Async XLA Ops:
  0.6 9.7 %copy-start = (bf16[256,128]{1,0:T(8,128)(2,1)S(1)}, bf16[256,128]{1,0:T(8,128)(2,1)}, u32[]{:S(2)}) copy-start(bf16[256,128]{1,0:T(8,128)(2,1)} %param.9) | copy-start | bytes 196612
  3.8 31.4 %all-to-all-start.2 = ((bf16[128,16,256]{0,2,1:T(8,128)(2,1)}), bf16[128,16,256]{0,2,1:T(8,128)(2,1)S(1)}, u32[]{:S(2)}, u32[]{:S(2)}) async-start(bf16[128,16,256]{0,2,1:T(8,128)(2,1)} %bitcast.11), calls=%async_computation.2 | async-start | bytes 2097152 | tf_op jit(solution)/shard_map/all_to_all | solution.py:108
  41.6 1.2 copy-start.4
  45.1 52.2 %all-to-all-start.3 = ((f32[16,128,256]{1,2,0:T(8,128)}), f32[16,128,256]{1,2,0:T(8,128)S(1)}, u32[]{:S(2)}, u32[]{:S(2)}) async-start(f32[16,128,256]{1,2,0:T(8,128)} %bitcast.49), calls=%async_computation.3 | async-start | bytes 4194304 | tf_op jit(solution)/shard_map/all_to_all | solution.py:128
  100.9 29.6 %all-to-all-start = ((bf16[128,16,256]{0,2,1:T(8,128)(2,1)}), bf16[128,16,256]{0,2,1:T(8,128)(2,1)S(1)}, u32[]{:S(2)}, u32[]{:S(2)}) async-start(bf16[128,16,256]{0,2,1:T(8,128)(2,1)} %bitcast.55), calls=%async_computation | async-start | bytes 2097152 | tf_op jit(solution)/shard_map/all_to_all | solution.py:107
  140.1 2.3 %copy-start.2 = (bf16[16,1,128,256]{2,3,0,1:T(8,128)(2,1)}, bf16[16,1,128,256]{2,3,0,1:T(8,128)(2,1)S(1)}, u32[]{:S(2)}) copy-start(bf16[16,1,128,256]{2,3,0,1:T(8,128)(2,1)S(1)} %copy.41) | copy-start | bytes 3145732
  144.0 52.4 %all-to-all-start.1 = ((f32[16,128,256]{1,2,0:T(8,128)}), f32[16,128,256]{1,2,0:T(8,128)}, u32[]{:S(2)}, u32[]{:S(2)}) async-start(f32[16,128,256]{1,2,0:T(8,128)} %bitcast.48), calls=%async_computation.1 | async-start | bytes 4194304 | tf_op jit(solution)/shard_map/all_to_all | solution.py:127
  148.8 2.4 %copy-start.1 = (bf16[128,4096]{0,1:T(8,128)(2,1)S(1)}, bf16[128,4096]{0,1:T(8,128)(2,1)}, u32[]{:S(2)}) copy-start(bf16[128,4096]{0,1:T(8,128)(2,1)} %get-tuple-element.36) | copy-start | bytes 3145732
  196.4 2.0 %copy-start.3 = (bf16[128,4096]{1,0:T(8,128)(2,1)S(1)}, bf16[128,4096]{1,0:T(8,128)(2,1)}, u32[]{:S(2)}) copy-start(bf16[128,4096]{1,0:T(8,128)(2,1)} %param.8) | copy-start | bytes 3145732
where the time goes:
time: 200 us
  waiting for transfers between devices  111 us (56%)
  local copies, waits for them, and re-layouts  35 us (18%)
  matrix products  21.1 us (11%)
  starting transfers between devices  21 us (10%)
  other arithmetic  11.1 us (6%)
    all_to_all x1, waiting for transfers between devices, shards(): lax.all_to_all(back_sum, 'ctx', split_axis=0, concat_axis=1, tiled=True)  42.9 us
    all_to_all x1, waiting for transfers between devices, shards(): lax.all_to_all(mixed_sum, 'ctx', split_axis=0, concat_axis=1, tiled=True)  34.5 us
    all_to_all x1, waiting for transfers between devices, shards(): lax.all_to_all(gated_grad, 'ctx', split_axis=1, concat_axis=0, tiled=True)  16.7 us
    all_to_all x1, waiting for transfers between devices, shards(): lax.all_to_all(product, 'ctx', split_axis=1, concat_axis=0, tiled=True)  16.6 us
    dot_general x2, matrix products, toeplitz(): jnp.einsum('gj,tsj->gts', filter_rows, selector, preferred_element_type=j...  16.3 us
    unnamed x16, local copies, waits for them, and re-layouts  10.6 us
    all_to_all x1, starting transfers between devices, shards(): lax.all_to_all(gated_grad, 'ctx', split_axis=1, concat_axis=0, tiled=True)  6.52 us
    all_to_all x1, starting transfers between devices, shards(): lax.all_to_all(back_sum, 'ctx', split_axis=0, concat_axis=1, tiled=True)  4.83 us
  transfers between devices with their start and end apart: 4, of which 4 were waited for; matrix products, arithmetic and copies ran while one was open for 17% of the time, Pallas kernels for 0%

commit v1 on v0

--- a/solution.py
+++ b/solution.py
@@ -6,6 +6,22 @@
 
 GSIZE = 16
 TAPS = 128
+
+
+def exchange_in_pairs(value, axis, split, join):
+    ways, here = (lax.axis_size(axis), lax.axis_index(axis))
+    width = value.shape[split] // ways
+    lengths = list(value.shape)
+    lengths[split] = width
+    height = lengths[join]
+    lengths[join] = height * ways
+    full = jnp.zeros(lengths, value.dtype)
+    for mask in range(ways):
+        part = lax.dynamic_slice_in_dim(value, (here ^ mask) * width, width, axis=split)
+        if mask:
+            part = lax.ppermute(part, axis, [(d, d ^ mask) for d in range(ways)])
+        full = lax.dynamic_update_slice_in_dim(full, part, (here ^ mask) * height, axis=join)
+    return full
 
 
 def toeplitz(filter_rows, offsets):
@@ -125,7 +141,7 @@
     back_sum = back_sum.reshape(total_rows, channels)
     mixed_home, back_home = (
         lax.all_to_all(mixed_sum, "ctx", split_axis=0, concat_axis=1, tiled=True),
-        lax.all_to_all(back_sum, "ctx", split_axis=0, concat_axis=1, tiled=True),
+        exchange_in_pairs(back_sum, "ctx", 0, 1),
     )
     grad_scale = 1.0 / math.sqrt(local_rows * lax.axis_size("ctx") * GSIZE)
     grad_query = (grad_out.astype(jnp.float32) * mixed_home).astype(jnp.bfloat16)

time: 200 us -> 209 us (1.045)
  starting transfers between devices: 21 us -> 34 us
  waiting for transfers between devices: 111 us -> 104 us
  local copies, waits for them, and re-layouts: 35 us -> 38.3 us
    all_to_all x1 -> x0, waiting for transfers between devices: 42.9 us -> none  [shards(): lax.all_to_all(back_sum, 'ctx', split_axis=0, concat_axis=1, tiled=True)]
    ppermute x0 -> x15, waiting for transfers between devices: none -> 36.5 us  [exchange_in_pairs(): part = lax.ppermute(part, axis, [(d, d ^ mask) for d in range(ways)])]
    ppermute x0 -> x15, starting transfers between devices: none -> 17.6 us  [exchange_in_pairs(): part = lax.ppermute(part, axis, [(d, d ^ mask) for d in range(ways)])]
    all_to_all x1 -> x0, starting transfers between devices: 4.83 us -> none  [shards(): lax.all_to_all(back_sum, 'ctx', split_axis=0, concat_axis=1, tiled=True)]
    unnamed x16 -> x21, local copies, waits for them, and re-layouts: 10.6 us -> 11.5 us
  transfers between devices with their start and end apart: 4 -> 18, of which waited for: 4 -> 11; matrix products, arithmetic and copies ran while one was open for 17% -> 17% of each run, Pallas kernels for 0% -> 0%
where the time goes in v1:
time: 209 us; the launch traced here: 208 us
  waiting for transfers between devices  104 us (50%)
  local copies, waits for them, and re-layouts  38.3 us (18%)
  starting transfers between devices  34 us (16%)
  matrix products  21.2 us (10%)
  other arithmetic  9.58 us (5%)
    ppermute x15, waiting for transfers between devices, exchange_in_pairs(): part = lax.ppermute(part, axis, [(d, d ^ mask) for d in range(ways)])  36.5 us
    all_to_all x1, waiting for transfers between devices, shards(): lax.all_to_all(mixed_sum, 'ctx', split_axis=0, concat_axis=1, tiled=True)  34.5 us
    ppermute x15, starting transfers between devices, exchange_in_pairs(): part = lax.ppermute(part, axis, [(d, d ^ mask) for d in range(ways)])  17.6 us
    all_to_all x1, waiting for transfers between devices, shards(): lax.all_to_all(gated_grad, 'ctx', split_axis=1, concat_axis=0, tiled=True)  16.7 us
    all_to_all x1, waiting for transfers between devices, shards(): lax.all_to_all(product, 'ctx', split_axis=1, concat_axis=0, tiled=True)  16.6 us
    dot_general x2, matrix products, toeplitz(): jnp.einsum('gj,tsj->gts', filter_rows, selector, preferred_element_type=j...  16.3 us
    unnamed x21, local copies, waits for them, and re-layouts  11.5 us
    all_to_all x1, starting transfers between devices, shards(): lax.all_to_all(gated_grad, 'ctx', split_axis=1, concat_axis=0, tiled=True)  6.52 us
  transfers between devices with their start and end apart: 18, of which 11 were waited for; matrix products, arithmetic and copies ran while one was open for 17% of the time, Pallas kernels for 0%

profile of v1, /device:TPU:15, one launch (start us, length us, event | category | flops | bytes accessed | tf_op | source)
XLA Modules:
  0.0 208.2 jit_solution(11612093982162679567)
XLA Ops:
  0.6 1.8 fusion.7
  2.5 1.3 copy.75
  3.8 6.5 %all-to-all-start.2 = ((bf16[128,16,256]{0,2,1:T(8,128)(2,1)}), bf16[128,16,256]{0,2,1:T(8,128)(2,1)S(1)}, u32[]{:S(2)}, u32[]{:S(2)}) async-start(bf16[128,16,256]{0,2,1:T(8,128)(2,1)} %bitcast.11), calls=%async_computation.2 | async-start | bytes 2097152 | tf_op jit(solution)/shard_map/all_to_all | solution.py:124
  10.3 8.2 %fusion.26 = bf16[16,128,256,1]{2,0,1,3:T(8,128)(2,1)} fusion(s32[128,256]{1,0:T(8,128)S(1)} %iota_subtract_fusion, bf16[256,128]{1,0:T(8,128)(2,1)S(1)} %copy-done, s32[]{:T(128)S(6)} %select_n.99), kind=kOutput, calls=%fused_computation.34 | convolution fusion | flops 138936320 | bytes 1183748 | tf_op jit(solution)/shard_map/while/body/eval_jaxpr/gj,tsj->gts/dot_general | solution.py:30
  18.5 16.7 %all-to-all-done.2 = bf16[128,16,256]{0,2,1:T(8,128)(2,1)S(1)} async-done(((bf16[128,16,256]{0,2,1:T(8,128)(2,1)}), bf16[128,16,256]{0,2,1:T(8,128)(2,1)S(1)}, u32[]{:S(2)}, u32[]{:S(2)}) %all-to-all-start.2) | async-done | bytes 1048608 | tf_op jit(solution)/shard_map/all_to_all | solution.py:124
  35.2 0.1 slice.27
  35.2 0.3 fusion.11
  35.5 2.1 reshape.107
  37.6 4.0 %slice.28 = bf16[16,1,128,256]{2,1,3,0:T(2,128)(2,1)S(1)} slice(bf16[16,2,128,256]{2,1,3,0:T(2,128)(2,1)} %reshape.107), slice={[0:16], [1:2], [0:128], [0:256]} | slice | bytes 2097152 | tf_op jit(solution)/shard_map/while/body/eval_jaxpr/slice | solution.py:71
  41.6 0.2 copy.92
  41.8 1.0 copy-done.6
  42.8 0.8 fusion.20
  43.6 0.7 copy.80
  44.3 0.9 copy.108
  45.2 0.1 broadcast_in_dim.17
  45.3 1.3 constant_dynamic-slice_fusion
  46.5 0.1 collective-permute-start
  46.7 0.3 collective-permute-start.1
  46.9 2.3 %copy.66 = bf16[128,4096]{0,1:T(8,128)(2,1)} copy(bf16[128,4096]{1,0:T(8,128)(2,1)} %param.6) | data formatting | bytes 2097152 | tf_op args[1]
  49.2 2.3 %copy.67 = bf16[128,4096]{0,1:T(8,128)(2,1)} copy(bf16[128,4096]{1,0:T(8,128)(2,1)} %param.7) | data formatting | bytes 2097152 | tf_op args[2]
  51.4 1.8 collective-permute-start.2
  53.2 1.5 collective-permute-start.4
  54.8 0.9 constant_dynamic-update-slice_fusion.13
  55.7 2.9 %collective-permute-start.6 = (f32[128,256]{0,1:T(8,128)}, f32[128,256]{0,1:T(8,128)S(1)}, u32[]{:S(2)}, u32[]{:S(2)}) collective-permute-start(f32[128,256]{0,1:T(8,128)} %get-tuple-element.46), channel_id=1, source_target_pairs={{0,7},{1,6},{2,5},{3,4},{4,3},{5,2},{6,1},{7,0},{8,15},{9,14},{10,... | collective-permute-start | bytes 393224 | tf_op jit(solution)/shard_map/ppermute | solution.py:22
  58.6 0.9 constant_dynamic-update-slice_fusion.12
  59.5 1.2 collective-permute-start.7
  60.8 1.3 collective-permute-start.8
  62.1 1.3 collective-permute-start.9
  63.4 3.7 %collective-permute-done.5 = f32[128,256]{0,1:T(8,128)S(1)} collective-permute-done((f32[128,256]{0,1:T(8,128)}, f32[128,256]{0,1:T(8,128)S(1)}, u32[]{:S(2)}, u32[]{:S(2)}) %collective-permute-start.5) | collective-permute-done | bytes 131104 | tf_op jit(solution)/shard_map/ppermute | solution.py:22
  67.1 5.0 %collective-permute-start.10 = (f32[128,256]{0,1:T(8,128)}, f32[128,256]{0,1:T(8,128)S(1)}, u32[]{:S(2)}, u32[]{:S(2)}) collective-permute-start(f32[128,256]{0,1:T(8,128)} %get-tuple-element.42), channel_id=1, source_target_pairs={{0,11},{1,10},{2,9},{3,8},{4,15},{5,14},{6,13},{7,12},{8,3},{9,2},... | collective-permute-start | bytes 393224 | tf_op jit(solution)/shard_map/ppermute | solution.py:22
  72.2 0.1 collective-permute-start.11
  72.3 1.2 collective-permute-start.12
  73.5 10.2 %collective-permute-done.8 = f32[128,256]{0,1:T(8,128)S(1)} collective-permute-done((f32[128,256]{0,1:T(8,128)}, f32[128,256]{0,1:T(8,128)S(1)}, u32[]{:S(2)}, u32[]{:S(2)}) %collective-permute-start.8) | collective-permute-done | bytes 131104 | tf_op jit(solution)/shard_map/ppermute | solution.py:22
  83.7 2.9 %collective-permute-done.9 = f32[128,256]{0,1:T(8,128)S(1)} collective-permute-done((f32[128,256]{0,1:T(8,128)}, f32[128,256]{0,1:T(8,128)S(1)}, u32[]{:S(2)}, u32[]{:S(2)}) %collective-permute-start.9) | collective-permute-done | bytes 131104 | tf_op jit(solution)/shard_map/ppermute | solution.py:22
  86.6 1.0 collective-permute-start.14
  87.6 4.5 %collective-permute-done.10 = f32[128,256]{0,1:T(8,128)S(1)} collective-permute-done((f32[128,256]{0,1:T(8,128)}, f32[128,256]{0,1:T(8,128)S(1)}, u32[]{:S(2)}, u32[]{:S(2)}) %collective-permute-start.10) | collective-permute-done | bytes 131104 | tf_op jit(solution)/shard_map/ppermute | solution.py:22
  92.1 6.4 %collective-permute-done.11 = f32[128,256]{0,1:T(8,128)S(1)} collective-permute-done((f32[128,256]{0,1:T(8,128)}, f32[128,256]{0,1:T(8,128)S(1)}, u32[]{:S(2)}, u32[]{:S(2)}) %collective-permute-start.11) | collective-permute-done | bytes 131104 | tf_op jit(solution)/shard_map/ppermute | solution.py:22
  98.5 3.1 %collective-permute-done.12 = f32[128,256]{0,1:T(8,128)S(1)} collective-permute-done((f32[128,256]{0,1:T(8,128)}, f32[128,256]{0,1:T(8,128)S(1)}, u32[]{:S(2)}, u32[]{:S(2)}) %collective-permute-start.12) | collective-permute-done | bytes 131104 | tf_op jit(solution)/shard_map/ppermute | solution.py:22
  101.6 2.8 %collective-permute-done.13 = f32[128,256]{0,1:T(8,128)S(1)} collective-permute-done((f32[128,256]{0,1:T(8,128)S(1)}, f32[128,256]{0,1:T(8,128)S(1)}, u32[]{:S(2)}, u32[]{:S(2)}) %collective-permute-start.13) | collective-permute-done | bytes 131104 | tf_op jit(solution)/shard_map/ppermute | solution.py:22
  104.5 2.8 %collective-permute-done.14 = f32[128,256]{0,1:T(8,128)S(1)} collective-permute-done((f32[128,256]{0,1:T(8,128)S(1)}, f32[128,256]{0,1:T(8,128)S(1)}, u32[]{:S(2)}, u32[]{:S(2)}) %collective-permute-start.14) | collective-permute-done | bytes 131104 | tf_op jit(solution)/shard_map/ppermute | solution.py:22
  107.3 2.1 fusion.8
  109.4 5.0 %all-to-all-start = ((bf16[128,16,256]{0,2,1:T(8,128)(2,1)}), bf16[128,16,256]{0,2,1:T(8,128)(2,1)S(1)}, u32[]{:S(2)}, u32[]{:S(2)}) async-start(bf16[128,16,256]{0,2,1:T(8,128)(2,1)} %bitcast.56), calls=%async_computation | async-start | bytes 2097152 | tf_op jit(solution)/shard_map/all_to_all | solution.py:123
  114.4 0.1 iota_subtract_fusion.1
  114.5 8.2 %fusion.25 = bf16[16,128,256,1]{2,0,1,3:T(8,128)(2,1)} fusion(s32[128,256]{1,0:T(8,128)S(1)} %iota_subtract_fusion.1, bf16[256,128]{1,0:T(8,128)(2,1)S(1)} %copy-done, s32[]{:T(128)S(6)} %select_n.99), kind=kOutput, calls=%fused_computation.33 | convolution fusion | flops 138936320 | bytes 1183748 | tf_op jit(solution)/shard_map/while/body/eval_jaxpr/gj,tsj->gts/dot_general | solution.py:30
  122.7 16.6 %all-to-all-done = bf16[128,16,256]{0,2,1:T(8,128)(2,1)S(1)} async-done(((bf16[128,16,256]{0,2,1:T(8,128)(2,1)}), bf16[128,16,256]{0,2,1:T(8,128)(2,1)S(1)}, u32[]{:S(2)}, u32[]{:S(2)}) %all-to-all-start) | async-done | bytes 1048608 | tf_op jit(solution)/shard_map/all_to_all | solution.py:123
  139.3 1.6 fusion.12
  140.9 3.9 %copy.68 = bf16[16,256,256]{2,1,0:T(8,128)(2,1)} copy(bf16[16,256,256]{1,2,0:T(8,128)(2,1)} %fusion.12) | data formatting | bytes 4194304 | tf_op jit(solution)/shard_map/while/body/eval_jaxpr/concatenate | solution.py:66
  144.8 2.3 %slice.26 = bf16[16,1,128,256]{3,2,1,0:T(8,128)(2,1)} slice(bf16[16,2,128,256]{3,2,1,0:T(8,128)(2,1)} %bitcast.53), slice={[0:16], [0:1], [0:128], [0:256]} | slice | bytes 2097152 | tf_op jit(solution)/shard_map/while/body/eval_jaxpr/slice | solution.py:70
  147.1 1.6 copy.69
  148.8 2.3 %fusion.17 = f32[16,128,16,16]{1,3,0,2:T(8,128)S(1)} fusion(bf16[16,128,256,1]{2,0,1,3:T(8,128)(2,1)} %fusion.25, bf16[16,128,16,16]{1,3,2,0:T(8,128)(2,1)S(1)} %bitcast.46, bf16[16,128,16,16]{1,3,2,0:T(8,128)(2,1)S(1)} %bitcast.54), kind=kOutput, calls=%fused_computation.29 | convolution fusion | flops 272629760 | bytes 5242880 | tf_op jit(solution)/shard_map/while/body/eval_jaxpr/gts,bsgc->btgc/dot_general | solution.py:48
  151.1 1.6 copy.73
  152.7 4.8 %all-to-all-start.1 = ((f32[16,128,256]{1,2,0:T(8,128)}), f32[16,128,256]{1,2,0:T(8,128)}, u32[]{:S(2)}, u32[]{:S(2)}) async-start(f32[16,128,256]{1,2,0:T(8,128)} %bitcast.49), calls=%async_computation.1 | async-start | bytes 4194304 | tf_op jit(solution)/shard_map/all_to_all | solution.py:143
  157.5 2.4 %copy.82 = bf16[128,4096]{1,0:T(8,128)(2,1)} copy(bf16[128,4096]{0,1:T(8,128)(2,1)} %get-tuple-element.36) | data formatting | bytes 2097152
  159.8 1.3 copy.83
  161.2 1.7 fusion.32
  162.9 1.2 copy.94
  164.1 0.1 pad.7
  164.3 3.6 %reshape.109 = f32[16,128,257]{2,1,0:T(8,128)} reshape(f32[16,32896]{1,0:T(8,128)S(1)} %pad.7) | data formatting | bytes 4210688 | tf_op jit(solution)/shard_map/while/body/eval_jaxpr/reshape | solution.py:56
  167.9 1.9 slice_reduce_fusion
  169.8 0.1 rev.5
  169.9 0.6 broadcast_multiply_fusion
  170.5 34.5 %all-to-all-done.1 = f32[16,128,256]{1,2,0:T(8,128)} async-done(((f32[16,128,256]{1,2,0:T(8,128)}), f32[16,128,256]{1,2,0:T(8,128)}, u32[]{:S(2)}, u32[]{:S(2)}) %all-to-all-start.1) | async-done | bytes 2097184 | tf_op jit(solution)/shard_map/all_to_all | solution.py:143
  205.0 2.0 copy.74
  207.0 1.2 fusion.6
  (39 shorter events, 0.4 us)
Async XLA Ops:
  0.6 9.7 %copy-start = (bf16[256,128]{1,0:T(8,128)(2,1)S(1)}, bf16[256,128]{1,0:T(8,128)(2,1)}, u32[]{:S(2)}) copy-start(bf16[256,128]{1,0:T(8,128)(2,1)} %param.9) | copy-start | bytes 196612
  3.8 31.4 %all-to-all-start.2 = ((bf16[128,16,256]{0,2,1:T(8,128)(2,1)}), bf16[128,16,256]{0,2,1:T(8,128)(2,1)S(1)}, u32[]{:S(2)}, u32[]{:S(2)}) async-start(bf16[128,16,256]{0,2,1:T(8,128)(2,1)} %bitcast.11), calls=%async_computation.2 | async-start | bytes 2097152 | tf_op jit(solution)/shard_map/all_to_all | solution.py:124
  41.6 1.2 copy-start.6
  46.5 8.1 %collective-permute-start = (f32[128,256]{0,1:T(8,128)}, f32[128,256]{0,1:T(8,128)}, u32[]{:S(2)}, u32[]{:S(2)}) collective-permute-start(f32[128,256]{0,1:T(8,128)} %get-tuple-element.52), channel_id=1, source_target_pairs={{0,1},{1,0},{2,3},{3,2},{4,5},{5,4},{6,7},{7,6},{8,9},{9,8},{10,11... | collective-permute-start | bytes 393224 | tf_op jit(solution)/shard_map/ppermute | solution.py:22
  46.7 9.0 %collective-permute-start.1 = (f32[128,256]{0,1:T(8,128)}, f32[128,256]{0,1:T(8,128)}, u32[]{:S(2)}, u32[]{:S(2)}) collective-permute-start(f32[128,256]{0,1:T(8,128)} %get-tuple-element.51), channel_id=1, source_target_pairs={{0,2},{1,3},{2,0},{3,1},{4,6},{5,7},{6,4},{7,5},{8,10},{9,11},{10,... | collective-permute-start | bytes 393224 | tf_op jit(solution)/shard_map/ppermute | solution.py:22
  51.4 55.8 %copy-start.1 = (bf16[128,4096]{0,1:T(8,128)(2,1)S(1)}, bf16[128,4096]{0,1:T(8,128)(2,1)}, u32[]{:S(2)}) copy-start(bf16[128,4096]{0,1:T(8,128)(2,1)} %copy.66) | copy-start | bytes 3145732
  51.4 55.8 %copy-start.2 = (bf16[128,4096]{0,1:T(8,128)(2,1)S(1)}, bf16[128,4096]{0,1:T(8,128)(2,1)}, u32[]{:S(2)}) copy-start(bf16[128,4096]{0,1:T(8,128)(2,1)} %copy.67) | copy-start | bytes 3145732
  51.4 8.1 %collective-permute-start.2 = (f32[128,256]{0,1:T(8,128)}, f32[128,256]{0,1:T(8,128)S(1)}, u32[]{:S(2)}, u32[]{:S(2)}) collective-permute-start(f32[128,256]{0,1:T(8,128)} %get-tuple-element.50), channel_id=1, source_target_pairs={{0,3},{1,2},{2,1},{3,0},{4,7},{5,6},{6,5},{7,4},{8,11},{9,10},{10,... | collective-permute-start | bytes 393224 | tf_op jit(solution)/shard_map/ppermute | solution.py:22
  53.2 7.6 %collective-permute-start.3 = (f32[128,256]{0,1:T(8,128)}, f32[128,256]{0,1:T(8,128)S(1)}, u32[]{:S(2)}, u32[]{:S(2)}) collective-permute-start(f32[128,256]{0,1:T(8,128)} %get-tuple-element.49), channel_id=1, source_target_pairs={{0,4},{1,5},{2,6},{3,7},{4,0},{5,1},{6,2},{7,3},{8,12},{9,13},{10,... | collective-permute-start | bytes 393224 | tf_op jit(solution)/shard_map/ppermute | solution.py:22
  53.2 8.9 %collective-permute-start.4 = (f32[128,256]{0,1:T(8,128)}, f32[128,256]{0,1:T(8,128)S(1)}, u32[]{:S(2)}, u32[]{:S(2)}) collective-permute-start(f32[128,256]{0,1:T(8,128)} %get-tuple-element.48), channel_id=1, source_target_pairs={{0,5},{1,4},{2,7},{3,6},{4,1},{5,0},{6,3},{7,2},{8,13},{9,12},{10,... | collective-permute-start | bytes 393224 | tf_op jit(solution)/shard_map/ppermute | solution.py:22
  54.7 12.4 %collective-permute-start.5 = (f32[128,256]{0,1:T(8,128)}, f32[128,256]{0,1:T(8,128)S(1)}, u32[]{:S(2)}, u32[]{:S(2)}) collective-permute-start(f32[128,256]{0,1:T(8,128)} %get-tuple-element.47), channel_id=1, source_target_pairs={{0,6},{1,7},{2,4},{3,5},{4,2},{5,3},{6,0},{7,1},{8,14},{9,15},{10,... | collective-permute-start | bytes 393224 | tf_op jit(solution)/shard_map/ppermute | solution.py:22
  55.7 16.5 %collective-permute-start.6 = (f32[128,256]{0,1:T(8,128)}, f32[128,256]{0,1:T(8,128)S(1)}, u32[]{:S(2)}, u32[]{:S(2)}) collective-permute-start(f32[128,256]{0,1:T(8,128)} %get-tuple-element.46), channel_id=1, source_target_pairs={{0,7},{1,6},{2,5},{3,4},{4,3},{5,2},{6,1},{7,0},{8,15},{9,14},{10,... | collective-permute-start | bytes 393224 | tf_op jit(solution)/shard_map/ppermute | solution.py:22
  59.5 12.7 %collective-permute-start.7 = (f32[128,256]{0,1:T(8,128)}, f32[128,256]{0,1:T(8,128)S(1)}, u32[]{:S(2)}, u32[]{:S(2)}) collective-permute-start(f32[128,256]{0,1:T(8,128)} %get-tuple-element.45), channel_id=1, source_target_pairs={{0,8},{1,9},{2,10},{3,11},{4,12},{5,13},{6,14},{7,15},{8,0},{9,1},... | collective-permute-start | bytes 393224 | tf_op jit(solution)/shard_map/ppermute | solution.py:22
  60.8 22.9 %collective-permute-start.8 = (f32[128,256]{0,1:T(8,128)}, f32[128,256]{0,1:T(8,128)S(1)}, u32[]{:S(2)}, u32[]{:S(2)}) collective-permute-start(f32[128,256]{0,1:T(8,128)} %get-tuple-element.44), channel_id=1, source_target_pairs={{0,9},{1,8},{2,11},{3,10},{4,13},{5,12},{6,15},{7,14},{8,1},{9,0},... | collective-permute-start | bytes 393224 | tf_op jit(solution)/shard_map/ppermute | solution.py:22
  62.1 24.5 %collective-permute-start.9 = (f32[128,256]{0,1:T(8,128)}, f32[128,256]{0,1:T(8,128)S(1)}, u32[]{:S(2)}, u32[]{:S(2)}) collective-permute-start(f32[128,256]{0,1:T(8,128)} %get-tuple-element.43), channel_id=1, source_target_pairs={{0,10},{1,11},{2,8},{3,9},{4,14},{5,15},{6,12},{7,13},{8,2},{9,3},... | collective-permute-start | bytes 393224 | tf_op jit(solution)/shard_map/ppermute | solution.py:22
  67.1 25.0 %collective-permute-start.10 = (f32[128,256]{0,1:T(8,128)}, f32[128,256]{0,1:T(8,128)S(1)}, u32[]{:S(2)}, u32[]{:S(2)}) collective-permute-start(f32[128,256]{0,1:T(8,128)} %get-tuple-element.42), channel_id=1, source_target_pairs={{0,11},{1,10},{2,9},{3,8},{4,15},{5,14},{6,13},{7,12},{8,3},{9,2},... | collective-permute-start | bytes 393224 | tf_op jit(solution)/shard_map/ppermute | solution.py:22
  72.2 26.3 %collective-permute-start.11 = (f32[128,256]{0,1:T(8,128)}, f32[128,256]{0,1:T(8,128)S(1)}, u32[]{:S(2)}, u32[]{:S(2)}) collective-permute-start(f32[128,256]{0,1:T(8,128)} %get-tuple-element.41), channel_id=1, source_target_pairs={{0,12},{1,13},{2,14},{3,15},{4,8},{5,9},{6,10},{7,11},{8,4},{9,5},... | collective-permute-start | bytes 393224 | tf_op jit(solution)/shard_map/ppermute | solution.py:22
  72.3 29.3 %collective-permute-start.12 = (f32[128,256]{0,1:T(8,128)}, f32[128,256]{0,1:T(8,128)S(1)}, u32[]{:S(2)}, u32[]{:S(2)}) collective-permute-start(f32[128,256]{0,1:T(8,128)} %get-tuple-element.40), channel_id=1, source_target_pairs={{0,13},{1,12},{2,15},{3,14},{4,9},{5,8},{6,11},{7,10},{8,5},{9,4},... | collective-permute-start | bytes 393224 | tf_op jit(solution)/shard_map/ppermute | solution.py:22
  83.7 20.8 %collective-permute-start.13 = (f32[128,256]{0,1:T(8,128)S(1)}, f32[128,256]{0,1:T(8,128)S(1)}, u32[]{:S(2)}, u32[]{:S(2)}) collective-permute-start(f32[128,256]{0,1:T(8,128)S(1)} %get-tuple-element.39), channel_id=1, source_target_pairs={{0,14},{1,15},{2,12},{3,13},{4,10},{5,11},{6,8},{7,9},{8,6},{9,7},... | collective-permute-start | bytes 393224 | tf_op jit(solution)/shard_map/ppermute | solution.py:22
  86.6 20.6 %collective-permute-start.14 = (f32[128,256]{0,1:T(8,128)S(1)}, f32[128,256]{0,1:T(8,128)S(1)}, u32[]{:S(2)}, u32[]{:S(2)}) collective-permute-start(f32[128,256]{0,1:T(8,128)S(1)} %get-tuple-element.38), channel_id=1, source_target_pairs={{0,15},{1,14},{2,13},{3,12},{4,11},{5,10},{6,9},{7,8},{8,7},{9,6},... | collective-permute-start | bytes 393224 | tf_op jit(solution)/shard_map/ppermute | solution.py:22
  109.4 29.9 %all-to-all-start = ((bf16[128,16,256]{0,2,1:T(8,128)(2,1)}), bf16[128,16,256]{0,2,1:T(8,128)(2,1)S(1)}, u32[]{:S(2)}, u32[]{:S(2)}) async-start(bf16[128,16,256]{0,2,1:T(8,128)(2,1)} %bitcast.56), calls=%async_computation | async-start | bytes 2097152 | tf_op jit(solution)/shard_map/all_to_all | solution.py:123
  148.8 2.3 %copy-start.4 = (bf16[16,1,128,256]{2,3,0,1:T(8,128)(2,1)}, bf16[16,1,128,256]{2,3,0,1:T(8,128)(2,1)S(1)}, u32[]{:S(2)}) copy-start(bf16[16,1,128,256]{2,3,0,1:T(8,128)(2,1)S(1)} %copy.69) | copy-start | bytes 3145732
  152.7 52.4 %all-to-all-start.1 = ((f32[16,128,256]{1,2,0:T(8,128)}), f32[16,128,256]{1,2,0:T(8,128)}, u32[]{:S(2)}, u32[]{:S(2)}) async-start(f32[16,128,256]{1,2,0:T(8,128)} %bitcast.49), calls=%async_computation.1 | async-start | bytes 4194304 | tf_op jit(solution)/shard_map/all_to_all | solution.py:143
  157.5 2.4 %copy-start.3 = (bf16[128,4096]{0,1:T(8,128)(2,1)S(1)}, bf16[128,4096]{0,1:T(8,128)(2,1)}, u32[]{:S(2)}) copy-start(bf16[128,4096]{0,1:T(8,128)(2,1)} %get-tuple-element.26) | copy-start | bytes 3145732
  205.0 2.0 copy-start.5
